TPU v7x, 32 devices: a whole 2x2x4 slice. The times are simulated.
32 devices in a mesh: row: 8 (over z, y), col: 4 (over x, core).
Axes of the slice: x: 2, y: 2, z: 4, core: 2. Of those that a mesh axis runs over, the one named last changes fastest.
Arguments:
- tokens_in: bfloat16 [192, 8192], P('row', 'col'), may hold values from -6 to 6
- gate_weight: bfloat16 [8192, 28672], P('col', 'row'), may hold values from -0.0625 to 0.0625
- up_weight: bfloat16 [8192, 28672], P('col', 'row'), may hold values from -0.0625 to 0.0625
- down_weight: bfloat16 [28672, 8192], P('row', 'col'), may hold values from -0.03125 to 0.03125
- out_grad: bfloat16 [192, 8192], P('row', 'col'), may hold values from -0.29882812 to 0.29882812
Outputs:
- output: bfloat16 [192, 8192], P('row', 'col')
- in_grad: bfloat16 [192, 8192], P('row', 'col')
- gate_grad: bfloat16 [8192, 28672], P('col', 'row')
- up_grad: bfloat16 [8192, 28672], P('col', 'row')
- down_grad: bfloat16 [28672, 8192], P('row', 'col')
All inputs are finite; a program needn't handle non-finite values.
Results may differ from a plain program's by a relative error of at most 0.0051.
Values may be sent and summed in bfloat16 or wider, within the bound.
A program may use at most 192 MiB of HBM per device.

v0:
```python
import jax
import jax.numpy as jnp
from jax import lax
from jax.sharding import PartitionSpec as P


def contract_last(left, right):
    return lax.dot_general(
        left, right, (((1,), (1,)), ((), ())), preferred_element_type=jnp.float32
    )


def contract_first(left, right):
    return lax.dot_general(
        left, right, (((0,), (0,)), ((), ())), preferred_element_type=jnp.float32
    )


def forward_gate(gate_pre, up_pre):
    sigma_gate = jax.nn.sigmoid(gate_pre)
    activated = gate_pre * sigma_gate
    hidden = (activated * up_pre).astype(jnp.bfloat16)
    return (hidden, sigma_gate, activated)


def backward_gate(d_hidden, gate_pre, up_pre, sigma_gate, activated):
    d_gate = (d_hidden * up_pre * sigma_gate * (1.0 + gate_pre * (1.0 - sigma_gate))).astype(
        jnp.bfloat16
    )
    d_up = (d_hidden * activated).astype(jnp.bfloat16)
    return (d_gate, d_up)


def shards(tokens_in, gate_weight, up_weight, down_weight, out_grad):
    inputs_all = lax.all_gather(tokens_in, "row", axis=0, tiled=True)
    gate_part = jnp.dot(inputs_all, gate_weight, preferred_element_type=jnp.float32)
    up_part = jnp.dot(inputs_all, up_weight, preferred_element_type=jnp.float32)
    gate_pre, up_pre = (
        lax.psum_scatter(gate_part, "col", scatter_dimension=0, tiled=True),
        lax.psum_scatter(up_part, "col", scatter_dimension=0, tiled=True),
    )
    hidden_share, sigma_gate, activated = forward_gate(gate_pre, up_pre)
    hidden_all = lax.all_gather(hidden_share, "col", axis=0, tiled=True)
    output = lax.psum_scatter(
        jnp.dot(hidden_all, down_weight, preferred_element_type=jnp.float32),
        "row",
        scatter_dimension=0,
        tiled=True,
    ).astype(jnp.bfloat16)
    grad_all = lax.all_gather(out_grad, "row", axis=0, tiled=True)
    dhid_part = contract_last(grad_all, down_weight)
    d_hidden = lax.psum_scatter(dhid_part, "col", scatter_dimension=0, tiled=True)
    d_gate, d_up = backward_gate(d_hidden, gate_pre, up_pre, sigma_gate, activated)
    d_gate_all, d_up_all = (
        lax.all_gather(d_gate, "col", axis=0, tiled=True),
        lax.all_gather(d_up, "col", axis=0, tiled=True),
    )
    in_grad = lax.psum_scatter(
        contract_last(d_gate_all, gate_weight) + contract_last(d_up_all, up_weight),
        "row",
        scatter_dimension=0,
        tiled=True,
    ).astype(jnp.bfloat16)
    gate_grad = contract_first(inputs_all, d_gate_all).astype(jnp.bfloat16)
    up_grad = contract_first(inputs_all, d_up_all).astype(jnp.bfloat16)
    down_grad = contract_first(hidden_all, grad_all).astype(jnp.bfloat16)
    return (output, in_grad, gate_grad, up_grad, down_grad)


def solution(mesh):
    in_specs = (P("row", "col"), P("col", "row"), P("col", "row"), P("row", "col"), P("row", "col"))
    out_specs = (
        P("row", "col"),
        P("row", "col"),
        P("col", "row"),
        P("col", "row"),
        P("row", "col"),
    )
    return jax.shard_map(shards, mesh=mesh, in_specs=in_specs, out_specs=out_specs, check_vma=False)
```

profile of v0, /device:TPU:0, one launch (start us, length us, event | category | flops | bytes accessed | tf_op | source)
XLA Modules:
  0.0 378.7 jit_solution(6762438291876996533)
XLA Ops:
  7.2 34.1 %all_gather.17 = bf16[192,2048]{1,0:T(8,128)(2,1)S(1)} all-gather(bf16[24,2048]{1,0:T(8,128)(2,1)} %param.9), channel_id=1, replica_groups=mesh['row'=8,'col'=4] {'row'}, dimensions={0}, use_global_device_ids=true | all-gather | bytes 884736 | tf_op jit(solution)/shard_map/all_gather | solution.py:50
  41.3 11.7 %fusion.6 = f32[192,3584]{1,0:T(8,128)} fusion(bf16[192,2048]{1,0:T(8,128)(2,1)S(1)} %all_gather.17, bf16[3584,2048]{1,0:T(8,128)(2,1)} %param.8), kind=kOutput, calls=%fused_computation.14 | convolution fusion | flops 2818572288 | bytes 18219008 | tf_op jit(solution)/shard_map/dot_general | solution.py:8
  53.1 0.8 copy-done.3
  53.9 32.1 %all_gather.15 = bf16[192,2048]{1,0:T(8,128)(2,1)S(1)} all-gather(bf16[24,2048]{1,0:T(8,128)(2,1)S(1)} %copy-done.3), channel_id=1, replica_groups=mesh['row'=8,'col'=4] {'row'}, dimensions={0}, use_global_device_ids=true | all-gather | bytes 884736 | tf_op jit(solution)/shard_map/all_gather | solution.py:35
  86.0 9.8 %fusion.3 = f32[192,3584]{1,0:T(8,128)} fusion(bf16[192,2048]{1,0:T(8,128)(2,1)S(1)} %all_gather.15, bf16[2048,3584]{1,0:T(8,128)(2,1)} %param.6), kind=kOutput, calls=%fused_computation.11 | convolution fusion | flops 2818572288 | bytes 18219008 | tf_op jit(solution)/shard_map/dot_general | solution.py:36
  95.8 9.7 %fusion.4 = f32[192,3584]{1,0:T(8,128)} fusion(bf16[192,2048]{1,0:T(8,128)(2,1)S(1)} %all_gather.15, bf16[2048,3584]{1,0:T(8,128)(2,1)} %param.7), kind=kOutput, calls=%fused_computation.12 | convolution fusion | flops 2818572288 | bytes 18219008 | tf_op jit(solution)/shard_map/dot_general | solution.py:37
  105.6 26.5 %reduce-scatter.6.cloned.1.call-done = f32[48,3584]{1,0:T(8,128)} async-done(((f32[192,3584]{1,0:T(8,128)}), f32[48,3584]{1,0:T(8,128)}) %reduce-scatter.6.cloned.1.call-update) | async-done | bytes 688144 | tf_op jit(solution)/shard_map/reduce_scatter | solution.py:39
  132.1 38.5 %reduce-scatter.8.cloned.1.call-done = f32[48,3584]{1,0:T(8,128)} async-done(((f32[192,3584]{1,0:T(8,128)}), f32[48,3584]{1,0:T(8,128)}) %reduce-scatter.8.cloned.1.call-update) | async-done | bytes 688144 | tf_op jit(solution)/shard_map/reduce_scatter | solution.py:40
  170.7 2.8 multiply_convert_fusion
  174.7 17.5 %all-gather.4.cloned.1.call-done = bf16[192,3584]{1,0:T(8,128)(2,1)} async-done(((bf16[48,3584]{1,0:T(8,128)(2,1)}), bf16[192,3584]{1,0:T(8,128)(2,1)}) %all-gather.4.cloned.1.call-update) | async-done | bytes 1376272 | tf_op jit(solution)/shard_map/all_gather | solution.py:43
  192.2 9.8 %fusion.5 = f32[192,2048]{1,0:T(8,128)} fusion(bf16[192,3584]{1,0:T(8,128)(2,1)} %all-gather.4.cloned.1.call-done, bf16[3584,2048]{1,0:T(8,128)(2,1)} %param.8), kind=kOutput, calls=%fused_computation.13 | convolution fusion | flops 2818572288 | bytes 17629184 | tf_op jit(solution)/shard_map/dot_general | solution.py:45
  202.2 10.5 %all-gather.6.cloned.1.call-done = bf16[192,3584]{1,0:T(8,128)(2,1)} async-done(((bf16[48,3584]{1,0:T(8,128)(2,1)}), bf16[192,3584]{1,0:T(8,128)(2,1)}) %all-gather.6.cloned.1.call-update) | async-done | bytes 1376272 | tf_op jit(solution)/shard_map/all_gather | solution.py:55
  212.7 8.5 %fusion.7 = f32[192,2048]{1,0:T(8,128)S(1)} fusion(bf16[192,3584]{1,0:T(8,128)(2,1)} %all-gather.6.cloned.1.call-done, bf16[2048,3584]{1,0:T(8,128)(2,1)} %param.6), kind=kOutput, calls=%fused_computation.15 | convolution fusion | flops 2818572288 | bytes 17629184 | tf_op jit(solution)/shard_map/dot_general | solution.py:8
  221.2 12.1 %all-gather.8.cloned.1.call-done = bf16[192,3584]{1,0:T(8,128)(2,1)} async-done(((bf16[48,3584]{1,0:T(8,128)(2,1)}), bf16[192,3584]{1,0:T(8,128)(2,1)}) %all-gather.8.cloned.1.call-update) | async-done | bytes 1376272 | tf_op jit(solution)/shard_map/all_gather | solution.py:56
  233.3 11.6 %convolution_add_fusion = f32[192,2048]{1,0:T(8,128)} fusion(f32[192,2048]{1,0:T(8,128)S(1)} %fusion.7, bf16[192,3584]{1,0:T(8,128)(2,1)} %all-gather.8.cloned.1.call-done, bf16[2048,3584]{1,0:T(8,128)(2,1)} %param.7), kind=kOutput, calls=%fused_computation.5 | convolution fusion | flops 2818965504 | bytes 19202048 | tf_op jit(solution)/shard_map/dot_general | solution.py:8
  244.9 1.3 copy-done.1
  246.2 7.6 %fusion = bf16[2048,3584]{0,1:T(8,128)(2,1)} fusion(bf16[192,3584]{1,0:T(8,128)(2,1)S(1)} %copy-done.1, bf16[192,2048]{1,0:T(8,128)(2,1)S(1)} %all_gather.15), kind=kOutput, calls=%fused_computation.3 | convolution fusion | flops 2825912320 | bytes 16842752 | tf_op jit(solution)/shard_map/dot_general | solution.py:14
  253.8 18.8 %copy.10 = bf16[2048,3584]{1,0:T(8,128)(2,1)} copy(bf16[2048,3584]{0,1:T(8,128)(2,1)} %fusion) | data formatting | bytes 29360128
  272.6 7.6 %fusion.1 = bf16[2048,3584]{0,1:T(8,128)(2,1)} fusion(bf16[192,3584]{1,0:T(8,128)(2,1)S(1)} %copy-done.2, bf16[192,2048]{1,0:T(8,128)(2,1)S(1)} %all_gather.15), kind=kOutput, calls=%fused_computation.4 | convolution fusion | flops 2825912320 | bytes 16842752 | tf_op jit(solution)/shard_map/dot_general | solution.py:14
  280.2 18.8 %copy.11 = bf16[2048,3584]{1,0:T(8,128)(2,1)} copy(bf16[2048,3584]{0,1:T(8,128)(2,1)} %fusion.1) | data formatting | bytes 29360128
  299.0 7.6 %convolution_convert_fusion = bf16[3584,2048]{1,0:T(8,128)(2,1)} fusion(bf16[192,3584]{1,0:T(8,128)(2,1)S(1)} %copy-done, bf16[192,2048]{1,0:T(8,128)(2,1)S(1)} %all_gather.17), kind=kOutput, calls=%fused_computation | convolution fusion | flops 2825912320 | bytes 16842752 | tf_op jit(solution)/shard_map/dot_general | solution.py:14
  306.6 1.6 convert_element_type.31
  308.2 62.1 %reduce-scatter.14.cloned.1.call-done = f32[24,2048]{1,0:T(8,128)} async-done(((f32[192,2048]{1,0:T(8,128)}), f32[24,2048]{1,0:T(8,128)}) %reduce-scatter.14.cloned.1.call-update) | async-done | bytes 196624 | tf_op jit(solution)/shard_map/reduce_scatter | solution.py:58
  370.3 1.6 convert_element_type.34
  (24 shorter events, 1.7 us)
Async XLA Ops:
  7.2 98.5 %reduce-scatter.12.cloned.1.call-start = ((), (), s32[]{:S(2)}) async-start(), calls=%async_computation.9 | async-start | bytes 3440640 | tf_op jit(solution)/shard_map/reduce_scatter | solution.py:52
  53.0 0.9 copy-start.3
  53.0 79.1 %reduce-scatter.6.cloned.1.call-start = ((), (), s32[]{:S(2)}) async-start(), calls=%async_computation.5 | async-start | bytes 3440640 | tf_op jit(solution)/shard_map/reduce_scatter | solution.py:39
  95.8 74.9 %reduce-scatter.8.cloned.1.call-start = ((), (), s32[]{:S(2)}) async-start(), calls=%async_computation.6 | async-start | bytes 3440640 | tf_op jit(solution)/shard_map/reduce_scatter | solution.py:40
  105.6 86.6 %all-gather.4.cloned.1.call-start = ((), (), s32[]{:S(2)}) async-start(), calls=%async_computation.7 | async-start | bytes 1720320 | tf_op jit(solution)/shard_map/all_gather | solution.py:43
  173.5 39.2 %all-gather.6.cloned.1.call-start = ((), (), s32[]{:S(2)}) async-start(), calls=%async_computation.10 | async-start | bytes 1720320 | tf_op jit(solution)/shard_map/all_gather | solution.py:55
  174.1 59.2 %all-gather.8.cloned.1.call-start = ((), (), s32[]{:S(2)}) async-start(), calls=%async_computation.11 | async-start | bytes 1720320 | tf_op jit(solution)/shard_map/all_gather | solution.py:56
  174.6 132.0 %reduce-scatter.10.cloned.1.call-start = ((), (), s32[]{:S(2)}) async-start(), calls=%async_computation.8 | async-start | bytes 1769472 | tf_op jit(solution)/shard_map/reduce_scatter | solution.py:44
  202.0 168.3 %reduce-scatter.14.cloned.1.call-start = ((), (), s32[]{:S(2)}) async-start(), calls=%async_computation.12 | async-start | bytes 1769472 | tf_op jit(solution)/shard_map/reduce_scatter | solution.py:58
  244.9 1.3 copy-start.1
  253.8 18.8 %copy-start.2 = (bf16[192,3584]{1,0:T(8,128)(2,1)S(1)}, bf16[192,3584]{1,0:T(8,128)(2,1)}, u32[]{:S(2)}) copy-start(bf16[192,3584]{1,0:T(8,128)(2,1)} %all-gather.8.cloned.1.call-done) | copy-start | bytes 4128772
  280.2 18.8 %copy-start = (bf16[192,3584]{1,0:T(8,128)(2,1)S(1)}, bf16[192,3584]{1,0:T(8,128)(2,1)}, u32[]{:S(2)}) copy-start(bf16[192,3584]{1,0:T(8,128)(2,1)} %all-gather.4.cloned.1.call-done) | copy-start | bytes 4128772
Sparse Core Ops, SparseCore 0:
  53.1 36.2 reduce-scatter.11
  95.9 36.1 reduce-scatter.5
  135.3 35.3 reduce-scatter.7
  173.6 18.5 all-gather.3
  194.1 18.5 all-gather.5
  214.7 18.5 all-gather.7
  236.7 65.4 reduce-scatter.9
  305.6 64.6 reduce-scatter.13
where the time goes:
time: 380 us; the launch traced here: 379 us
  waiting for transfers between devices  168 us (44%)
  matrix products  83.8 us (22%)
  blocking collectives  66.2 us (17%)
  local copies, waits for them, and re-layouts  39.7 us (10%)
  between operations  14.2 us (4%)
  other arithmetic  5.93 us (2%)
    reduce_scatter x1, waiting for transfers between devices, shards(): lax.psum_scatter(contract_last(d_gate_all, gate_weight) + contract_last(d...  62.1 us
    unnamed x10, local copies, waits for them, and re-layouts  39.7 us
    reduce_scatter x1, waiting for transfers between devices, shards(): lax.psum_scatter(up_part, 'col', scatter_dimension=0, tiled=True)  38.5 us
    all_gather x1, blocking collectives, shards(): grad_all = lax.all_gather(out_grad, 'row', axis=0, tiled=True)  34.1 us
    all_gather x1, blocking collectives, shards(): inputs_all = lax.all_gather(tokens_in, 'row', axis=0, tiled=True)  32.1 us
    dot_general x3, matrix products, contract_last(): lax.dot_general(left, right, (((1,), (1,)), ((), ())), preferred_element_...  31.8 us
    reduce_scatter x1, waiting for transfers between devices, shards(): lax.psum_scatter(gate_part, 'col', scatter_dimension=0, tiled=True)  26.5 us
    dot_general x3, matrix products, contract_first(): lax.dot_general(left, right, (((0,), (0,)), ((), ())), preferred_element_...  22.8 us
  transfers between devices with their start and end apart: 8, of which 6 were waited for; matrix products, arithmetic and copies ran while one was open for 29% of the time, Pallas kernels for 0%

commit v1 on v0

--- a/solution.py
+++ b/solution.py
@@ -2,6 +2,23 @@
 import jax.numpy as jnp
 from jax import lax
 from jax.sharding import PartitionSpec as P
+
+
+def in_order(blocks, dim):
+    dims = list(blocks.shape[1:])
+    dims[dim] *= blocks.shape[0]
+    return jnp.moveaxis(blocks, 0, dim).reshape(dims)
+
+
+def gather_around(value, axis, dim):
+    count = lax.axis_size(axis)
+    right = [(i, (i + 1) % count) for i in range(count)]
+    blocks = [value]
+    while len(blocks) < count:
+        blocks.append(lax.ppermute(blocks[-1], axis, right))
+    index = lax.axis_index(axis)
+    blocks = jnp.stack(blocks)[(index - jnp.arange(count)) % count]
+    return in_order(blocks, dim)
 
 
 def contract_last(left, right):
@@ -47,7 +64,7 @@
         scatter_dimension=0,
         tiled=True,
     ).astype(jnp.bfloat16)
-    grad_all = lax.all_gather(out_grad, "row", axis=0, tiled=True)
+    grad_all = gather_around(out_grad, "row", 0)
     dhid_part = contract_last(grad_all, down_weight)
     d_hidden = lax.psum_scatter(dhid_part, "col", scatter_dimension=0, tiled=True)
     d_gate, d_up = backward_gate(d_hidden, gate_pre, up_pre, sigma_gate, activated)

time: 380 us -> 374 us (0.984)
  blocking collectives: 66.2 us -> 34.1 us
  waiting for transfers between devices: 168 us -> 192 us
    ppermute x0 -> x7, waiting for transfers between devices: none -> 50.5 us  [gather_around(): blocks.append(lax.ppermute(blocks[-1], axis, right))]
    reduce_scatter x1, waiting for transfers between devices: 38.5 us -> 0.02 us  [shards(): lax.psum_scatter(up_part, 'col', scatter_dimension=0, tiled=True)]
    reduce_scatter x1, waiting for transfers between devices: 0.02 us -> 38.1 us  [shards(): lax.psum_scatter(dhid_part, 'col', scatter_dimension=0, tiled=True)]
    all_gather x1 -> x0, blocking collectives: 34.1 us -> none  [shards(): grad_all = lax.all_gather(out_grad, 'row', axis=0, tiled=True)]
    reduce_scatter x1, waiting for transfers between devices: 26.5 us -> 0.02 us  [shards(): lax.psum_scatter(gate_part, 'col', scatter_dimension=0, tiled=True)]
    unnamed x10 -> x17, local copies, waits for them, and re-layouts: 39.7 us -> 39.8 us
  transfers between devices with their start and end apart: 8 -> 15, of which waited for: 6 -> 12; matrix products, arithmetic and copies ran while one was open for 29% -> 31% of each run, Pallas kernels for 0% -> 0%
where the time goes in v1:
time: 374 us; the launch traced here: 373 us
  waiting for transfers between devices  192 us (51%)
  matrix products  83.9 us (22%)
  local copies, waits for them, and re-layouts  40.4 us (11%)
  blocking collectives  34.1 us (9%)
  between operations  14.2 us (4%)
  other arithmetic  5.95 us (2%)
    reduce_scatter x1, waiting for transfers between devices, shards(): lax.psum_scatter(contract_last(d_gate_all, gate_weight) + contract_last(d...  62.2 us
    ppermute x7, waiting for transfers between devices, gather_around(): blocks.append(lax.ppermute(blocks[-1], axis, right))  50.5 us
    unnamed x17, local copies, waits for them, and re-layouts  39.8 us
    reduce_scatter x1, waiting for transfers between devices, shards(): lax.psum_scatter(dhid_part, 'col', scatter_dimension=0, tiled=True)  38.1 us
    all_gather x1, blocking collectives, shards(): inputs_all = lax.all_gather(tokens_in, 'row', axis=0, tiled=True)  34.1 us
    dot_general x3, matrix products, contract_last(): lax.dot_general(left, right, (((1,), (1,)), ((), ())), preferred_element_...  31.9 us
    dot_general x3, matrix products, contract_first(): lax.dot_general(left, right, (((0,), (0,)), ((), ())), preferred_element_...  22.8 us
    all_gather x1, waiting for transfers between devices, shards(): hidden_all = lax.all_gather(hidden_share, 'col', axis=0, tiled=True)  17.3 us
  transfers between devices with their start and end apart: 15, of which 12 were waited for; matrix products, arithmetic and copies ran while one was open for 31% of the time, Pallas kernels for 0%

profile of v1, /device:TPU:0, one launch (start us, length us, event | category | flops | bytes accessed | tf_op | source)
XLA Modules:
  0.0 372.6 jit_solution(15795913255214046446)
XLA Ops:
  7.2 34.1 %all_gather.12 = bf16[192,2048]{1,0:T(8,128)(2,1)S(1)} all-gather(bf16[24,2048]{1,0:T(8,128)(2,1)} %param.5), channel_id=1, replica_groups=mesh['row'=8,'col'=4] {'row'}, dimensions={0}, use_global_device_ids=true | all-gather | bytes 884736 | tf_op jit(solution)/shard_map/all_gather | solution.py:52
  41.3 9.7 %fusion.5 = f32[192,3584]{1,0:T(8,128)} fusion(bf16[192,2048]{1,0:T(8,128)(2,1)S(1)} %all_gather.12, bf16[2048,3584]{1,0:T(8,128)(2,1)} %param.6), kind=kOutput, calls=%fused_computation.27 | convolution fusion | flops 2818572288 | bytes 18219008 | tf_op jit(solution)/shard_map/dot_general | solution.py:53
  51.1 9.7 %fusion.6 = f32[192,3584]{1,0:T(8,128)} fusion(bf16[192,2048]{1,0:T(8,128)(2,1)S(1)} %all_gather.12, bf16[2048,3584]{1,0:T(8,128)(2,1)} %param.7), kind=kOutput, calls=%fused_computation.28 | convolution fusion | flops 2818572288 | bytes 18219008 | tf_op jit(solution)/shard_map/dot_general | solution.py:54
  63.3 6.7 %collective-permute-done = bf16[24,2048]{1,0:T(8,128)(2,1)S(1)} collective-permute-done((bf16[24,2048]{1,0:T(8,128)(2,1)S(1)}, bf16[24,2048]{1,0:T(8,128)(2,1)S(1)}, u32[]{:S(2)}, u32[]{:S(2)}) %collective-permute-start) | collective-permute-done | bytes 98336 | tf_op jit(solution)/shard_map/ppermute | solution.py:18
  70.0 7.4 %collective-permute-done.1 = bf16[24,2048]{1,0:T(8,128)(2,1)S(1)} collective-permute-done((bf16[24,2048]{1,0:T(8,128)(2,1)S(1)}, bf16[24,2048]{1,0:T(8,128)(2,1)S(1)}, u32[]{:S(2)}, u32[]{:S(2)}) %collective-permute-start.1) | collective-permute-done | bytes 98336 | tf_op jit(solution)/shard_map/ppermute | solution.py:18
  77.4 7.3 %collective-permute-done.2 = bf16[24,2048]{1,0:T(8,128)(2,1)S(1)} collective-permute-done((bf16[24,2048]{1,0:T(8,128)(2,1)S(1)}, bf16[24,2048]{1,0:T(8,128)(2,1)S(1)}, u32[]{:S(2)}, u32[]{:S(2)}) %collective-permute-start.2) | collective-permute-done | bytes 98336 | tf_op jit(solution)/shard_map/ppermute | solution.py:18
  84.7 7.3 %collective-permute-done.3 = bf16[24,2048]{1,0:T(8,128)(2,1)S(1)} collective-permute-done((bf16[24,2048]{1,0:T(8,128)(2,1)S(1)}, bf16[24,2048]{1,0:T(8,128)(2,1)S(1)}, u32[]{:S(2)}, u32[]{:S(2)}) %collective-permute-start.3) | collective-permute-done | bytes 98336 | tf_op jit(solution)/shard_map/ppermute | solution.py:18
  92.0 7.3 %collective-permute-done.4 = bf16[24,2048]{1,0:T(8,128)(2,1)S(1)} collective-permute-done((bf16[24,2048]{1,0:T(8,128)(2,1)S(1)}, bf16[24,2048]{1,0:T(8,128)(2,1)S(1)}, u32[]{:S(2)}, u32[]{:S(2)}) %collective-permute-start.4) | collective-permute-done | bytes 98336 | tf_op jit(solution)/shard_map/ppermute | solution.py:18
  99.3 7.3 %collective-permute-done.5 = bf16[24,2048]{1,0:T(8,128)(2,1)S(1)} collective-permute-done((bf16[24,2048]{1,0:T(8,128)(2,1)S(1)}, bf16[24,2048]{1,0:T(8,128)(2,1)S(1)}, u32[]{:S(2)}, u32[]{:S(2)}) %collective-permute-start.5) | collective-permute-done | bytes 98336 | tf_op jit(solution)/shard_map/ppermute | solution.py:18
  106.6 7.3 %collective-permute-done.6 = bf16[24,2048]{1,0:T(8,128)(2,1)S(1)} collective-permute-done((bf16[24,2048]{1,0:T(8,128)(2,1)S(1)}, bf16[24,2048]{1,0:T(8,128)(2,1)S(1)}, u32[]{:S(2)}, u32[]{:S(2)}) %collective-permute-start.6) | collective-permute-done | bytes 98336 | tf_op jit(solution)/shard_map/ppermute | solution.py:18
  114.5 11.8 %fusion.8 = f32[192,3584]{1,0:T(8,128)} fusion(bf16[192,2048]{1,0:T(8,128)(2,1)S(1)} %bitcast.41, bf16[3584,2048]{1,0:T(8,128)(2,1)} %param.8), kind=kOutput, calls=%fused_computation.30 | convolution fusion | flops 2818572288 | bytes 18219008 | tf_op jit(solution)/shard_map/dot_general | solution.py:25
  126.4 38.1 %reduce-scatter.12.cloned.1.call-done = f32[48,3584]{1,0:T(8,128)} async-done(((f32[192,3584]{1,0:T(8,128)}), f32[48,3584]{1,0:T(8,128)}) %reduce-scatter.12.cloned.1.call-update) | async-done | bytes 688144 | tf_op jit(solution)/shard_map/reduce_scatter | solution.py:69
  168.7 17.3 %all-gather.4.cloned.1.call-done = bf16[192,3584]{1,0:T(8,128)(2,1)} async-done(((bf16[48,3584]{1,0:T(8,128)(2,1)}), bf16[192,3584]{1,0:T(8,128)(2,1)}) %all-gather.4.cloned.1.call-update) | async-done | bytes 1376272 | tf_op jit(solution)/shard_map/all_gather | solution.py:60
  186.0 9.8 %fusion.7 = f32[192,2048]{1,0:T(8,128)} fusion(bf16[192,3584]{1,0:T(8,128)(2,1)} %all-gather.4.cloned.1.call-done, bf16[3584,2048]{1,0:T(8,128)(2,1)} %param.8), kind=kOutput, calls=%fused_computation.29 | convolution fusion | flops 2818572288 | bytes 17629184 | tf_op jit(solution)/shard_map/dot_general | solution.py:62
  195.8 10.7 %all-gather.6.cloned.1.call-done = bf16[192,3584]{1,0:T(8,128)(2,1)} async-done(((bf16[48,3584]{1,0:T(8,128)(2,1)}), bf16[192,3584]{1,0:T(8,128)(2,1)}) %all-gather.6.cloned.1.call-update) | async-done | bytes 1376272 | tf_op jit(solution)/shard_map/all_gather | solution.py:72
  206.5 8.5 %fusion.9 = f32[192,2048]{1,0:T(8,128)S(1)} fusion(bf16[192,3584]{1,0:T(8,128)(2,1)} %all-gather.6.cloned.1.call-done, bf16[2048,3584]{1,0:T(8,128)(2,1)} %param.6), kind=kOutput, calls=%fused_computation.31 | convolution fusion | flops 2818572288 | bytes 17629184 | tf_op jit(solution)/shard_map/dot_general | solution.py:25
  215.0 12.1 %all-gather.8.cloned.1.call-done = bf16[192,3584]{1,0:T(8,128)(2,1)} async-done(((bf16[48,3584]{1,0:T(8,128)(2,1)}), bf16[192,3584]{1,0:T(8,128)(2,1)}) %all-gather.8.cloned.1.call-update) | async-done | bytes 1376272 | tf_op jit(solution)/shard_map/all_gather | solution.py:73
  227.1 11.6 %convolution_add_fusion = f32[192,2048]{1,0:T(8,128)} fusion(f32[192,2048]{1,0:T(8,128)S(1)} %fusion.9, bf16[192,3584]{1,0:T(8,128)(2,1)} %all-gather.8.cloned.1.call-done, bf16[2048,3584]{1,0:T(8,128)(2,1)} %param.7), kind=kOutput, calls=%fused_computation.6 | convolution fusion | flops 2818965504 | bytes 19202048 | tf_op jit(solution)/shard_map/dot_general | solution.py:25
  240.0 7.6 %fusion = bf16[2048,3584]{0,1:T(8,128)(2,1)} fusion(bf16[192,3584]{1,0:T(8,128)(2,1)S(1)} %copy-done.1, bf16[192,2048]{1,0:T(8,128)(2,1)S(1)} %all_gather.12), kind=kOutput, calls=%fused_computation.4 | convolution fusion | flops 2825912320 | bytes 16842752 | tf_op jit(solution)/shard_map/dot_general | solution.py:31
  247.6 18.9 %copy.10 = bf16[2048,3584]{1,0:T(8,128)(2,1)} copy(bf16[2048,3584]{0,1:T(8,128)(2,1)} %fusion) | data formatting | bytes 29360128
  266.5 7.6 %fusion.1 = bf16[2048,3584]{0,1:T(8,128)(2,1)} fusion(bf16[192,3584]{1,0:T(8,128)(2,1)S(1)} %copy-done.2, bf16[192,2048]{1,0:T(8,128)(2,1)S(1)} %all_gather.12), kind=kOutput, calls=%fused_computation.5 | convolution fusion | flops 2825912320 | bytes 16842752 | tf_op jit(solution)/shard_map/dot_general | solution.py:31
  274.1 18.8 %copy.11 = bf16[2048,3584]{1,0:T(8,128)(2,1)} copy(bf16[2048,3584]{0,1:T(8,128)(2,1)} %fusion.1) | data formatting | bytes 29360128
  292.8 7.6 %convolution_convert_fusion = bf16[3584,2048]{1,0:T(8,128)(2,1)} fusion(bf16[192,3584]{1,0:T(8,128)(2,1)S(1)} %copy-done, bf16[192,2048]{1,0:T(8,128)(2,1)S(1)} %bitcast.42), kind=kOutput, calls=%fused_computation.1 | convolution fusion | flops 2825912320 | bytes 16842752 | tf_op jit(solution)/shard_map/dot_general | solution.py:31
  302.0 62.2 %reduce-scatter.14.cloned.1.call-done = f32[24,2048]{1,0:T(8,128)} async-done(((f32[192,2048]{1,0:T(8,128)}), f32[24,2048]{1,0:T(8,128)}) %reduce-scatter.14.cloned.1.call-update) | async-done | bytes 196624 | tf_op jit(solution)/shard_map/reduce_scatter | solution.py:75
  (48 shorter events, 12.0 us)
Async XLA Ops:
  7.2 119.2 %reduce-scatter.6.cloned.1.call-start = ((), (), s32[]{:S(2)}) async-start(), calls=%async_computation.5 | async-start | bytes 3440640 | tf_op jit(solution)/shard_map/reduce_scatter | solution.py:56
  51.0 75.4 %reduce-scatter.8.cloned.1.call-start = ((), (), s32[]{:S(2)}) async-start(), calls=%async_computation.6 | async-start | bytes 3440640 | tf_op jit(solution)/shard_map/reduce_scatter | solution.py:57
  60.8 0.9 copy-start.3
  60.8 103.7 %reduce-scatter.12.cloned.1.call-start = ((), (), s32[]{:S(2)}) async-start(), calls=%async_computation.9 | async-start | bytes 3440640 | tf_op jit(solution)/shard_map/reduce_scatter | solution.py:69
  61.7 8.2 %collective-permute-start = (bf16[24,2048]{1,0:T(8,128)(2,1)S(1)}, bf16[24,2048]{1,0:T(8,128)(2,1)S(1)}, u32[]{:S(2)}, u32[]{:S(2)}) collective-permute-start(bf16[24,2048]{1,0:T(8,128)(2,1)S(1)} %copy-done.3), channel_id=1, source_target_pairs={{0,4},{4,8},{8,12},{12,16},{16,20},{20,24},{24,28},{28,0},{1,5},{5... | collective-permute-start | bytes 294920 | tf_op jit(solution)/shard_map/ppermute | solution.py:18
  70.0 7.4 %collective-permute-start.1 = (bf16[24,2048]{1,0:T(8,128)(2,1)S(1)}, bf16[24,2048]{1,0:T(8,128)(2,1)S(1)}, u32[]{:S(2)}, u32[]{:S(2)}) collective-permute-start(bf16[24,2048]{1,0:T(8,128)(2,1)S(1)} %collective-permute-done), channel_id=1, source_target_pairs={{0,4},{4,8},{8,12},{12,16},{16,20},{20,24},{24,28},{28,0},{1,5},{5... | collective-permute-start | bytes 294920 | tf_op jit(solution)/shard_map/ppermute | solution.py:18
  77.3 7.3 %collective-permute-start.2 = (bf16[24,2048]{1,0:T(8,128)(2,1)S(1)}, bf16[24,2048]{1,0:T(8,128)(2,1)S(1)}, u32[]{:S(2)}, u32[]{:S(2)}) collective-permute-start(bf16[24,2048]{1,0:T(8,128)(2,1)S(1)} %collective-permute-done.1), channel_id=1, source_target_pairs={{0,4},{4,8},{8,12},{12,16},{16,20},{20,24},{24,28},{28,0},{1,5},{5... | collective-permute-start | bytes 294920 | tf_op jit(solution)/shard_map/ppermute | solution.py:18
  84.7 7.3 %collective-permute-start.3 = (bf16[24,2048]{1,0:T(8,128)(2,1)S(1)}, bf16[24,2048]{1,0:T(8,128)(2,1)S(1)}, u32[]{:S(2)}, u32[]{:S(2)}) collective-permute-start(bf16[24,2048]{1,0:T(8,128)(2,1)S(1)} %collective-permute-done.2), channel_id=1, source_target_pairs={{0,4},{4,8},{8,12},{12,16},{16,20},{20,24},{24,28},{28,0},{1,5},{5... | collective-permute-start | bytes 294920 | tf_op jit(solution)/shard_map/ppermute | solution.py:18
  92.0 7.3 %collective-permute-start.4 = (bf16[24,2048]{1,0:T(8,128)(2,1)S(1)}, bf16[24,2048]{1,0:T(8,128)(2,1)S(1)}, u32[]{:S(2)}, u32[]{:S(2)}) collective-permute-start(bf16[24,2048]{1,0:T(8,128)(2,1)S(1)} %collective-permute-done.3), channel_id=1, source_target_pairs={{0,4},{4,8},{8,12},{12,16},{16,20},{20,24},{24,28},{28,0},{1,5},{5... | collective-permute-start | bytes 294920 | tf_op jit(solution)/shard_map/ppermute | solution.py:18
  99.3 7.3 %collective-permute-start.5 = (bf16[24,2048]{1,0:T(8,128)(2,1)S(1)}, bf16[24,2048]{1,0:T(8,128)(2,1)S(1)}, u32[]{:S(2)}, u32[]{:S(2)}) collective-permute-start(bf16[24,2048]{1,0:T(8,128)(2,1)S(1)} %collective-permute-done.4), channel_id=1, source_target_pairs={{0,4},{4,8},{8,12},{12,16},{16,20},{20,24},{24,28},{28,0},{1,5},{5... | collective-permute-start | bytes 294920 | tf_op jit(solution)/shard_map/ppermute | solution.py:18
  106.6 7.3 %collective-permute-start.6 = (bf16[24,2048]{1,0:T(8,128)(2,1)S(1)}, bf16[24,2048]{1,0:T(8,128)(2,1)S(1)}, u32[]{:S(2)}, u32[]{:S(2)}) collective-permute-start(bf16[24,2048]{1,0:T(8,128)(2,1)S(1)} %collective-permute-done.5), channel_id=1, source_target_pairs={{0,4},{4,8},{8,12},{12,16},{16,20},{20,24},{24,28},{28,0},{1,5},{5... | collective-permute-start | bytes 294920 | tf_op jit(solution)/shard_map/ppermute | solution.py:18
  126.3 59.6 %all-gather.4.cloned.1.call-start = ((), (), s32[]{:S(2)}) async-start(), calls=%async_computation.7 | async-start | bytes 1720320 | tf_op jit(solution)/shard_map/all_gather | solution.py:60
  167.3 39.2 %all-gather.6.cloned.1.call-start = ((), (), s32[]{:S(2)}) async-start(), calls=%async_computation.10 | async-start | bytes 1720320 | tf_op jit(solution)/shard_map/all_gather | solution.py:72
  167.9 59.2 %all-gather.8.cloned.1.call-start = ((), (), s32[]{:S(2)}) async-start(), calls=%async_computation.11 | async-start | bytes 1720320 | tf_op jit(solution)/shard_map/all_gather | solution.py:73
  168.5 132.0 %reduce-scatter.10.cloned.1.call-start = ((), (), s32[]{:S(2)}) async-start(), calls=%async_computation.8 | async-start | bytes 1769472 | tf_op jit(solution)/shard_map/reduce_scatter | solution.py:61
  195.8 168.4 %reduce-scatter.14.cloned.1.call-start = ((), (), s32[]{:S(2)}) async-start(), calls=%async_computation.12 | async-start | bytes 1769472 | tf_op jit(solution)/shard_map/reduce_scatter | solution.py:75
  238.7 1.3 copy-start.1
  247.6 18.9 %copy-start.2 = (bf16[192,3584]{1,0:T(8,128)(2,1)S(1)}, bf16[192,3584]{1,0:T(8,128)(2,1)}, u32[]{:S(2)}) copy-start(bf16[192,3584]{1,0:T(8,128)(2,1)} %all-gather.8.cloned.1.call-done) | copy-start | bytes 4128772
  274.1 18.8 %copy-start = (bf16[192,3584]{1,0:T(8,128)(2,1)S(1)}, bf16[192,3584]{1,0:T(8,128)(2,1)}, u32[]{:S(2)}) copy-start(bf16[192,3584]{1,0:T(8,128)(2,1)} %all-gather.4.cloned.1.call-done) | copy-start | bytes 4128772
Sparse Core Ops, SparseCore 0:
  51.2 36.2 reduce-scatter.5
  90.6 35.3 reduce-scatter.7
  129.1 35.3 reduce-scatter.11
  167.4 18.5 all-gather.3
  188.0 18.5 all-gather.5
  208.5 18.5 all-gather.7
  230.5 65.7 reduce-scatter.9
  299.7 64.4 reduce-scatter.13
